TPU v7x, 32 devices: a whole 2x2x4 slice. The times are simulated.
32 devices in a mesh: stream: 2 (over core), dp: 16 (over z, y, x).
Axes of the slice: x: 2, y: 2, z: 4, core: 2. Of those that a mesh axis runs over, the one named last changes fastest.
Arguments:
- layer_input: bfloat16 [2, 16384, 768], P('stream', 'dp'), may hold values from -6 to 6
- pair_group: int32 [256], P('dp'), may hold values from 0 to 108, as said below
- query_weight: bfloat16 [768, 768], replicated, may hold values from -0.21875 to 0.21875
- query_bias: float32 [768], replicated, may hold values from -4 to 4
- key_weight: bfloat16 [768, 768], replicated, may hold values from -0.21875 to 0.21875
- value_weight: bfloat16 [768, 768], replicated, may hold values from -0.21875 to 0.21875
- value_bias: float32 [768], replicated, may hold values from -4 to 4
- out_weight: bfloat16 [768, 768], replicated, may hold values from -1 to 1
- out_bias: float32 [768], replicated, may hold values from -4 to 4
- mixer_gain: float32 [768], replicated, may hold values from 0.1 to 1.9
- mixer_shift: float32 [768], replicated, may hold values from -4 to 4
- up_weight: bfloat16 [768, 3072], replicated, may hold values from -0.21875 to 0.21875
- up_bias: float32 [3072], replicated, may hold values from -4 to 4
- down_weight: bfloat16 [3072, 768], replicated, may hold values from -0.109375 to 0.109375
- down_bias: float32 [768], replicated, may hold values from -4 to 4
- final_gain: float32 [768], replicated, may hold values from 0.1 to 1.9
- final_shift: float32 [768], replicated, may hold values from -4 to 4
- upstream: bfloat16 [2, 16384, 768], P('stream', 'dp'), may hold values from -0.75 to 0.75
Outputs:
- layer_output: bfloat16 [2, 16384, 768], P('stream', 'dp')
- input_grad: float32 [2, 16384, 768], P('stream', 'dp')
- total_loss: float32 [2, 256], P('stream', 'dp')
- query_weight_grad: float32 [768, 768], replicated
- query_bias_grad: float32 [768], replicated
- key_weight_grad: float32 [768, 768], replicated
- value_weight_grad: float32 [768, 768], replicated
- value_bias_grad: float32 [768], replicated
- out_weight_grad: float32 [768, 768], replicated
- out_bias_grad: float32 [768], replicated
- mixer_gain_grad: float32 [768], replicated
- mixer_shift_grad: float32 [768], replicated
- up_weight_grad: float32 [768, 3072], replicated
- up_bias_grad: float32 [3072], replicated
- down_weight_grad: float32 [3072, 768], replicated
- down_bias_grad: float32 [768], replicated
- final_gain_grad: float32 [768], replicated
- final_shift_grad: float32 [768], replicated
Inputs may be any that keep to these rules, and one draw needn't show every extreme that they name: `pair_group`: every one of the 109 ids names 2 or more pairs; the first and the last pair have the same id.
All inputs are finite; a program needn't handle non-finite values.
Results may differ from a plain program's by a relative error of at most 0.014.
Values may be sent and summed in bfloat16 or wider, within the bound.
No kernel may reach another device: no remote copies, remote signals or barrier semaphores. Data moves between devices by JAX's collectives and lax.ppermute only.
A program may use at most 256 MiB of HBM per device.

v0:
```python
import math
import jax
import jax.numpy as jnp
from jax import lax
from jax.sharding import PartitionSpec as P

D = 768
HEADS = 12
HD = 64
GROUPS = 109
MARGIN = 0.3
LOGIT_SCALE = 30.0
NORM_EPS = 1e-12
UNIT_EPS = 1e-06
highest = lax.Precision.HIGHEST


def norm_forward(values, gain, shift):
    centred = values - jnp.mean(values, axis=-1, keepdims=True)
    inv_std = lax.rsqrt(jnp.mean(centred * centred, axis=-1, keepdims=True) + NORM_EPS)
    normed_hat = centred * inv_std
    return (normed_hat * gain + shift, normed_hat, inv_std)


def norm_backward(grad_out, normed_hat, inv_std, gain):
    grad_hat = grad_out * gain
    mean_grad = jnp.mean(grad_hat, axis=-1, keepdims=True)
    mean_cross = jnp.mean(grad_hat * normed_hat, axis=-1, keepdims=True)
    grad_in = inv_std * (grad_hat - mean_grad - normed_hat * mean_cross)
    return (grad_in, jnp.sum(grad_out * normed_hat, axis=0), jnp.sum(grad_out, axis=0))


def gelu_slope(values):
    normal_cdf = 0.5 * (1.0 + lax.erf(values * (1.0 / math.sqrt(2.0))))
    return normal_cdf + values * jnp.exp(-0.5 * values * values) * (1.0 / math.sqrt(2.0 * math.pi))


def to_heads(matrix, key_span):
    return matrix.reshape(-1, key_span, HEADS, HD)


def attend_scores(query_heads, key_heads, key_mask, factor):
    raw_scores = (
        jnp.einsum("bqhd,bkhd->bhqk", query_heads, key_heads, preferred_element_type=jnp.float32)
        * factor
    )
    return jnp.where(key_mask, raw_scores, -jnp.inf)


def outer_sum(left, right):
    return jnp.einsum("ri,rj->ij", left, right, preferred_element_type=jnp.float32)


def back_project(grad_rows, weight):
    return jnp.einsum("re,de->rd", grad_rows, weight, preferred_element_type=jnp.float32)


def shards(
    layer_input,
    pair_group,
    query_weight,
    query_bias,
    key_weight,
    value_weight,
    value_bias,
    out_weight,
    out_bias,
    mixer_gain,
    mixer_shift,
    up_weight,
    up_bias,
    down_weight,
    down_bias,
    final_gain,
    final_shift,
    upstream,
):
    tokens = layer_input[0]
    token_count = tokens.shape[0]
    seq_count = pair_group.shape[0]
    seq_len = token_count // seq_count
    key_span = 2 * seq_len
    factor = 1.0 / math.sqrt(HD)
    place = jnp.arange(key_span) // seq_len
    key_mask = place[:, None] == place[None, :]
    queries = (
        jnp.dot(tokens, query_weight, preferred_element_type=jnp.float32) + query_bias
    ).astype(jnp.bfloat16)
    keys_all = jnp.dot(tokens, key_weight, preferred_element_type=jnp.float32).astype(jnp.bfloat16)
    values_all = (
        jnp.dot(tokens, value_weight, preferred_element_type=jnp.float32) + value_bias
    ).astype(jnp.bfloat16)
    query_heads = to_heads(queries, key_span)
    key_heads = to_heads(keys_all, key_span)
    value_heads = to_heads(values_all, key_span)
    scores = attend_scores(query_heads, key_heads, key_mask, factor)
    row_top = jnp.max(scores, axis=-1, keepdims=True)
    log_total = row_top + jnp.log(jnp.sum(jnp.exp(scores - row_top), axis=-1, keepdims=True))
    probs_low = jnp.exp(scores - log_total).astype(jnp.bfloat16)
    context = jnp.einsum(
        "bhqk,bkhd->bqhd", probs_low, value_heads, preferred_element_type=jnp.float32
    )
    context = context.astype(jnp.bfloat16).reshape(token_count, D)
    attended = jnp.dot(context, out_weight, preferred_element_type=jnp.float32) + out_bias
    normed, hat_one, inv_one = norm_forward(
        tokens.astype(jnp.float32) + attended, mixer_gain, mixer_shift
    )
    normed_low = normed.astype(jnp.bfloat16)
    hidden_pre = jnp.dot(normed_low, up_weight, preferred_element_type=jnp.float32) + up_bias
    activated = jax.nn.gelu(hidden_pre, approximate=False).astype(jnp.bfloat16)
    branch = jnp.dot(activated, down_weight, preferred_element_type=jnp.float32) + down_bias
    final_rows, hat_two, inv_two = norm_forward(normed + branch, final_gain, final_shift)
    layer_output = final_rows.astype(jnp.bfloat16)[None]
    lead_rows = final_rows.reshape(seq_count, seq_len, D)[:, 0, :]
    lead_inv = lax.rsqrt(jnp.sum(lead_rows * lead_rows, axis=-1, keepdims=True) + UNIT_EPS)
    unit_rows = (lead_rows * lead_inv).astype(jnp.bfloat16)
    pairs_all = seq_count * lax.axis_size("dp")
    all_groups = lax.all_gather(pair_group, "dp", axis=0, tiled=True)
    everyone = lax.all_gather(unit_rows, ("stream", "dp"), axis=0, tiled=True).reshape(
        2, pairs_all, D
    )
    half_index = lax.axis_index("stream")
    offset = lax.axis_index("dp") * seq_count
    others = lax.dynamic_index_in_dim(everyone, 1 - half_index, 0, keepdims=False)
    group_range = jnp.arange(GROUPS, dtype=jnp.int32)
    own_hits = (pair_group[:, None] == group_range[None, :]).astype(jnp.float32)
    counts = lax.psum(jnp.sum(own_hits, axis=0), "dp")
    row_weight = pairs_all / GROUPS / jnp.sum(own_hits * counts[None, :], axis=1)
    sim_scores = LOGIT_SCALE * jnp.einsum(
        "id,jd->ij", unit_rows, others, preferred_element_type=jnp.float32
    )
    columns = jnp.arange(pairs_all, dtype=jnp.int32)
    diagonal = columns[None, :] == (offset + jnp.arange(seq_count, dtype=jnp.int32))[:, None]
    same_group = pair_group[:, None] == all_groups[None, :]
    logits = sim_scores - LOGIT_SCALE * MARGIN * diagonal.astype(jnp.float32)
    masked = jnp.where(same_group, logits, -jnp.inf)
    loss_top = jnp.max(masked, axis=1, keepdims=True)
    exp_terms = jnp.exp(masked - loss_top)
    row_sums = jnp.sum(exp_terms, axis=1, keepdims=True)
    own_logit = jnp.sum(jnp.where(diagonal, logits, 0.0), axis=1)
    row_loss = loss_top[:, 0] + jnp.log(row_sums[:, 0]) - own_logit
    loss_rows = (row_weight * row_loss)[None]
    dlogits = row_weight[:, None] * (exp_terms / row_sums - diagonal.astype(jnp.float32))
    grad_own = LOGIT_SCALE * jnp.dot(dlogits, others.astype(jnp.float32), precision=highest)
    grad_cols = LOGIT_SCALE * jnp.dot(dlogits.T, unit_rows.astype(jnp.float32), precision=highest)
    grad_terms = jnp.zeros((2, pairs_all, D), jnp.float32)
    grad_terms = lax.dynamic_update_slice(grad_terms, grad_cols[None], (1 - half_index, 0, 0))
    grad_terms = lax.dynamic_update_slice(grad_terms, grad_own[None], (half_index, offset, 0))
    unit_grad = lax.psum_scatter(
        grad_terms.reshape(2 * pairs_all, D), ("stream", "dp"), scatter_dimension=0, tiled=True
    )
    cross = jnp.sum(lead_rows * unit_grad, axis=-1, keepdims=True)
    lead_grad = lead_inv * unit_grad - lead_inv * lead_inv * lead_inv * cross * lead_rows
    final_grad = upstream[0].astype(jnp.float32).reshape(seq_count, seq_len, D)
    final_grad = final_grad.at[:, 0, :].add(lead_grad).reshape(token_count, D)
    dresid_two, final_gain_grad, final_shift_grad = norm_backward(
        final_grad, hat_two, inv_two, final_gain
    )
    dbranch = dresid_two.astype(jnp.bfloat16)
    down_weight_grad = outer_sum(activated, dbranch)
    down_bias_grad = jnp.sum(dbranch, axis=0, dtype=jnp.float32)
    dpre = (back_project(dbranch, down_weight) * gelu_slope(hidden_pre)).astype(jnp.bfloat16)
    up_weight_grad = outer_sum(normed_low, dpre)
    up_bias_grad = jnp.sum(dpre, axis=0, dtype=jnp.float32)
    dnormed = dresid_two + back_project(dpre, up_weight)
    dresid_one, mixer_gain_grad, mixer_shift_grad = norm_backward(
        dnormed, hat_one, inv_one, mixer_gain
    )
    datt = dresid_one.astype(jnp.bfloat16)
    out_weight_grad = outer_sum(context, datt)
    out_bias_grad = jnp.sum(datt, axis=0, dtype=jnp.float32)
    dcontext = back_project(datt, out_weight).astype(jnp.bfloat16)
    dcontext_heads = to_heads(dcontext, key_span)
    again = attend_scores(query_heads, key_heads, key_mask, factor)
    probs_f = jnp.exp(again - log_total)
    dprobs = jnp.einsum(
        "bqhd,bkhd->bhqk", dcontext_heads, value_heads, preferred_element_type=jnp.float32
    )
    row_dot = jnp.sum(probs_f * dprobs, axis=-1, keepdims=True)
    dscores = (probs_f * (dprobs - row_dot)).astype(jnp.bfloat16)
    dqueries = (
        jnp.einsum("bhqk,bkhd->bqhd", dscores, key_heads, preferred_element_type=jnp.float32)
        * factor
    )
    dqueries = dqueries.astype(jnp.bfloat16).reshape(token_count, D)
    dkeys = (
        jnp.einsum("bhqk,bqhd->bkhd", dscores, query_heads, preferred_element_type=jnp.float32)
        * factor
    )
    dkeys = dkeys.astype(jnp.bfloat16).reshape(token_count, D)
    dvalues = (
        jnp.einsum(
            "bhqk,bqhd->bkhd",
            probs_f.astype(jnp.bfloat16),
            dcontext_heads,
            preferred_element_type=jnp.float32,
        )
        .astype(jnp.bfloat16)
        .reshape(token_count, D)
    )
    query_weight_grad = outer_sum(tokens, dqueries)
    query_bias_grad = jnp.sum(dqueries, axis=0, dtype=jnp.float32)
    key_weight_grad = outer_sum(tokens, dkeys)
    value_weight_grad = outer_sum(tokens, dvalues)
    value_bias_grad = jnp.sum(dvalues, axis=0, dtype=jnp.float32)
    input_grad = (
        dresid_one
        + back_project(dqueries, query_weight)
        + back_project(dkeys, key_weight)
        + back_project(dvalues, value_weight)
    )
    local_grads = [
        query_weight_grad,
        query_bias_grad,
        key_weight_grad,
        value_weight_grad,
        value_bias_grad,
        out_weight_grad,
        out_bias_grad,
        mixer_gain_grad,
        mixer_shift_grad,
        up_weight_grad,
        up_bias_grad,
        down_weight_grad,
        down_bias_grad,
        final_gain_grad,
        final_shift_grad,
    ]
    flat_grads = jnp.concatenate([piece.reshape(-1) for piece in local_grads])
    total_len = flat_grads.shape[0]
    share_devices = lax.axis_size(("stream", "dp"))
    share_count = -(-total_len // share_devices)
    share_width = -(-share_count // 128) * 128
    flat_grads = flat_grads.reshape(share_devices, share_count)
    flat_grads = jnp.pad(flat_grads, ((0, 0), (0, share_width - share_count))).reshape(-1, 128)
    shares = lax.psum_scatter(flat_grads, ("stream", "dp"), scatter_dimension=0, tiled=True)
    reduced = lax.all_gather(
        shares.astype(jnp.bfloat16), ("stream", "dp"), axis=0, tiled=True
    ).astype(shares.dtype)
    reduced = reduced.reshape(share_devices, share_width)[:, :share_count].reshape(-1)
    summed = []
    cursor = 0
    for piece in local_grads:
        piece_len = piece.size
        summed.append(reduced[cursor : cursor + piece_len].reshape(piece.shape))
        cursor = cursor + piece_len
    return (
        layer_output,
        input_grad[None],
        loss_rows,
        summed[0],
        summed[1],
        summed[2],
        summed[3],
        summed[4],
        summed[5],
        summed[6],
        summed[7],
        summed[8],
        summed[9],
        summed[10],
        summed[11],
        summed[12],
        summed[13],
        summed[14],
    )


def solution(mesh):
    return jax.shard_map(
        shards,
        mesh=mesh,
        in_specs=(
            P("stream", "dp", None),
            P("dp"),
            P(),
            P(),
            P(),
            P(),
            P(),
            P(),
            P(),
            P(),
            P(),
            P(),
            P(),
            P(),
            P(),
            P(),
            P(),
            P("stream", "dp", None),
        ),
        out_specs=(
            P("stream", "dp", None),
            P("stream", "dp", None),
            P("stream", "dp"),
            P(),
            P(),
            P(),
            P(),
            P(),
            P(),
            P(),
            P(),
            P(),
            P(),
            P(),
            P(),
            P(),
            P(),
            P(),
        ),
        check_vma=False,
    )
```

profile of v0, /device:TPU:0, one launch (start us, length us, event | category | flops | bytes accessed | tf_op | source)
XLA Modules:
  0.0 1631.6 jit_solution(9747999156966175325)
XLA Ops:
  8.5 43.5 %psum.7 = f32[109]{0:T(128)S(1)} all-reduce(f32[109]{0:T(128)S(1)} %convert_reduce_fusion.5), channel_id=1, replica_groups=mesh['stream'=2,'dp'=16] {'dp'}, use_global_device_ids=true, to_apply=%region_8.9 | all-reduce | flops 109 | bytes 872 | tf_op jit(solution)/shard_map/psum | solution.py:127
  56.1 9.0 all-reduce.1
  65.3 4.3 add_convert_fusion
  81.4 3.1 copy.99
  97.9 34.5 %fusion.3 = (bf16[1024,3072]{1,0:T(8,128)(2,1)S(1)}, f32[1024,3072]{1,0:T(8,128)}) fusion(f32[3072]{0:T(1024)S(1)} %copy-done.61, bf16[768,3072]{1,0:T(8,128)(2,1)S(1)} %bitcast.204, f32[1024,768]{1,0:T(8,128)S(1)} %get-tuple-element.63, f32[768]{0:T(1024)S(1)} %copy-done.37, f32[768]{0:T(1024)S(1)} %copy-done.32, f32[1024]{0:T(1024)S(1)} %add_rsqrt_fusion.1, ...), kind=kOutput, calls=%fused_computation.6 | convolution fusion | flops 5043388416 | bytes 26765312 | tf_op jit(solution)/shard_map/dot_general | solution.py:109
  132.5 5.5 fusion.100
  141.3 69.7 %all_gather.10 = bf16[512,768]{1,0:T(8,128)(2,1)S(1)} all-gather(bf16[16,768]{1,0:T(8,128)(2,1)S(1)} %fusion.71), channel_id=1, replica_groups=mesh['stream'=2,'dp'=16] {'stream','dp'}, dimensions={0}, use_global_device_ids=true | all-gather | bytes 811008 | tf_op jit(solution)/shard_map/all_gather | solution.py:119
  215.9 3.4 convert.3
  219.3 93.5 %reduce-scatter.4.cloned.1.call-done = f32[16,768]{1,0:T(8,128)} async-done(((f32[512,768]{1,0:T(8,128)}), f32[16,768]{1,0:T(8,128)}) %reduce-scatter.4.cloned.1.call-update) | async-done | bytes 49168 | tf_op jit(solution)/shard_map/reduce_scatter | solution.py:149
  317.9 4.5 fusion.19
  323.4 4.1 convert_reduce_fusion.1
  327.6 10.3 fusion.86
  337.9 12.5 convert_reduce_fusion
  350.4 6.5 multiply_reduce_fusion.1
  356.9 8.9 convolution_bitcast_fusion
  375.1 6.4 convert_reduce_fusion.3
  386.1 4.9 fusion.41
  393.1 10.8 reshape.345
  404.0 9.6 copy.134
  422.9 3.0 copy.120
  426.0 3.2 reshape.342
  429.2 3.9 copy.114
  438.4 3.0 copy.118
  441.4 3.2 reshape.340
  444.6 4.7 convolution_bitcast_fusion.2
  449.3 3.0 copy.119
  452.4 3.2 reshape.341
  455.6 3.3 constant_dynamic-update-slice_fusion.9
  460.2 21.3 %dynamic-update-slice.6 = f32[7087104]{0:T(1024)} dynamic-update-slice(f32[7087104]{0:T(1024)} %constant_dynamic-update-slice_fusion.8, f32[589824]{0:T(1024)} %reshape.341, s32[]{} %constant.180) | dynamic-update-slice | bytes 4718596
  481.5 21.2 %dynamic-update-slice.7 = f32[7087104]{0:T(1024)} dynamic-update-slice(f32[7087104]{0:T(1024)} %dynamic-update-slice.6, f32[589824]{0:T(1024)} %reshape.342, s32[]{} %constant.181) | dynamic-update-slice | bytes 4718596
  504.0 20.3 %dynamic-update-slice.9 = f32[7087104]{0:T(1024)} dynamic-update-slice(f32[7087104]{0:T(1024)} %constant_dynamic-update-slice_fusion.7, f32[589824]{0:T(1024)S(1)} %reshape.343, s32[]{} %constant.183) | dynamic-update-slice | bytes 4718596
  528.2 80.3 %dynamic-update-slice.13 = f32[7087104]{0:T(1024)} dynamic-update-slice(f32[7087104]{0:T(1024)} %constant_dynamic-update-slice_fusion.4, f32[2359296]{0:T(1024)} %bitcast.172, s32[]{} %constant.187) | dynamic-update-slice | bytes 18874372
  609.9 80.8 %dynamic-update-slice.15 = f32[7087104]{0:T(1024)} dynamic-update-slice(f32[7087104]{0:T(1024)} %constant_dynamic-update-slice_fusion.3, f32[2359296]{0:T(1024)} %reshape.345, s32[]{} %constant.189) | dynamic-update-slice | bytes 18874372
  694.5 37.8 %reshape.346 = f32[32,221472]{1,0:T(8,128)} reshape(f32[7087104]{0:T(1024)} %constant_dynamic-update-slice_fusion) | data formatting | bytes 56696832 | tf_op jit(solution)/shard_map/reshape | solution.py:234
  732.3 20.9 %pad.6 = f32[32,221568]{1,0:T(8,128)} pad(f32[32,221472]{1,0:T(8,128)} %reshape.346, f32[]{:T(128)} %constant.120.clone.1), padding=0_0x0_96 | pad | bytes 56709124 | tf_op jit(solution)/shard_map/jit(_pad)/pad | solution.py:235
  753.2 25.4 %reshape.347 = f32[55392,128]{1,0:T(8,128)} reshape(f32[32,221568]{1,0:T(8,128)} %pad.6) | data formatting | bytes 56721408 | tf_op jit(solution)/shard_map/reshape | solution.py:235
  778.7 605.0 %fusion = f32[1744,128]{1,0:T(8,128)S(1)} fusion(f32[55392,128]{1,0:T(8,128)} %reshape.347), kind=kCustom, calls=%all-reduce-scatter | all-reduce-scatter fusion | flops 7143425 | bytes 29253632
  1385.0 3.1 collective-permute-done
  1396.1 3.3 add_bitcast_fusion
  1399.4 96.9 %all-gather.3.cloned.1.call-done = bf16[32,1731,128]{2,1,0:T(8,128)(2,1)} async-done(((bf16[1,1731,128]{2,1,0:T(8,128)(2,1)}), bf16[32,1731,128]{2,1,0:T(8,128)(2,1)}) %all-gather.3.cloned.1.call-update) | async-done | bytes 14180368 | tf_op jit(solution)/shard_map/all_gather | solution.py:237
  1496.2 12.8 copy.209
  1509.0 9.7 slice_convert_fusion
  1518.8 36.5 %reshape.361 = f32[7087104]{0:T(1024)} reshape(f32[32,221472]{1,0:T(8,128)} %slice_convert_fusion) | data formatting | bytes 56696832
  1558.0 8.3 slice.115
  1566.3 31.3 %slice.87 = f32[9228,768]{1,0:T(8,128)} reshape(f32[7087104]{0:T(1024)} %reshape.361) | data formatting | bytes 56696832 | tf_op jit(solution)/shard_map/slice | solution.py:245
  1597.6 8.1 slice.117
  1605.7 7.7 fusion.97
  1613.3 11.0 reshape.350
  (243 shorter events, 98.0 us)
Async XLA Ops:
  7.2 86.2 %copy-start = (bf16[768,768]{1,0:T(8,128)(2,1)S(1)}, bf16[768,768]{1,0:T(8,128)(2,1)}, u32[]{:S(2)}) copy-start(bf16[768,768]{1,0:T(8,128)(2,1)} %param.27) | copy-start | bytes 3538948
  7.2 305.6 %reduce-scatter.4.cloned.1.call-start = ((), (), s32[]{:S(2)}) async-start(), calls=%async_computation.1 | async-start | bytes 1622016 | tf_op jit(solution)/shard_map/reduce_scatter | solution.py:149
  65.2 24.6 %copy-start.29 = (pred[128,128]{0,1:T(8,128)(4,1)}, pred[128,128]{0,1:T(8,128)(4,1)S(1)}, u32[]{:S(2)}) copy-start(pred[128,128]{0,1:T(8,128)(4,1)S(1)} %broadcast_compare_fusion) | copy-start | bytes 49156
  69.6 3.4 copy-start.63
  78.9 11.0 copy-start.9
  93.5 39.0 %slice-start.2 = ((s8[4718592]{0:T(1024)(128)(4,1)}), s8[4194304]{0:T(1024)(128)(4,1)S(1)}, s32[]{:S(2)}) async-start(s8[4718592]{0:T(1024)(128)(4,1)} %bitcast.199), calls=%async_computation.5 | async-start | bytes 8388608
  95.2 37.2 %copy-start.5 = (f32[1024,768]{1,0:T(8,128)}, f32[1024,768]{1,0:T(8,128)S(1)}, u32[]{:S(2)}) copy-start(f32[1024,768]{1,0:T(8,128)S(1)} %get-tuple-element.63) | copy-start | bytes 9437188
  97.9 34.6 %slice-start.3 = ((s8[4718592]{0:T(1024)(128)(4,1)}), s8[524288]{0:T(1024)(128)(4,1)S(1)}, s32[]{:S(2)}) async-start(s8[4718592]{0:T(1024)(128)(4,1)} %bitcast.199), calls=%async_computation.6 | async-start | bytes 1048576
  97.9 34.6 %copy-start.65 = (f32[768]{0:T(1024)S(1)}, f32[768]{0:T(1024)}, u32[]{:S(2)}) copy-start(f32[768]{0:T(1024)} %param.34) | copy-start | bytes 9220
  132.4 5.5 copy-start.66
  138.7 72.3 %copy-start.39 = (s32[256]{0:T(256)S(1)}, s32[256]{0:T(256)}, u32[]{:S(2)}) copy-start(s32[256]{0:T(256)} %all-reduce.1) | copy-start | bytes 3076
  138.7 72.3 %copy-start.44 = (s32[16]{0:T(128)S(1)}, s32[16]{0:T(128)}, u32[]{:S(2)}) copy-start(s32[16]{0:T(128)} %param.21) | copy-start | bytes 196
  138.7 72.3 %copy-start.45 = (s32[16]{0:T(128)S(1)}, s32[16]{0:T(128)}, u32[]{:S(2)}) copy-start(s32[16]{0:T(128)} %iota_add_fusion) | copy-start | bytes 196
  138.7 72.8 %copy-start.53 = (f32[16]{0:T(128)S(1)}, f32[16]{0:T(128)}, u32[]{:S(2)}) copy-start(f32[16]{0:T(128)} %select_reduce_fusion.1) | copy-start | bytes 196
  140.5 71.6 %copy-start.18 = (f32[16,1,768]{2,1,0:T(1,128)}, f32[16,1,768]{2,1,0:T(1,128)S(1)}, u32[]{:S(2)}) copy-start(f32[16,1,768]{2,1,0:T(1,128)S(1)} %slice.104) | copy-start | bytes 147460
  141.2 70.9 %copy-start.46 = (f32[16]{0:T(128)}, f32[16]{0:T(128)S(1)}, u32[]{:S(2)}) copy-start(f32[16]{0:T(128)S(1)} %add_rsqrt_fusion.2) | copy-start | bytes 196
  141.3 70.8 %copy-start.31 = (bf16[16,768]{1,0:T(8,128)(2,1)}, bf16[16,768]{1,0:T(8,128)(2,1)S(1)}, u32[]{:S(2)}) copy-start(bf16[16,768]{1,0:T(8,128)(2,1)S(1)} %fusion.71) | copy-start | bytes 73732
  214.7 98.1 %copy-start.19 = (f32[16,1,768]{2,1,0:T(1,128)S(1)}, f32[16,1,768]{2,1,0:T(1,128)}, u32[]{:S(2)}) copy-start(f32[16,1,768]{2,1,0:T(1,128)} %copy-done.18) | copy-start | bytes 147460
  214.7 99.1 %copy-start.52 = (f32[16]{0:T(128)S(1)}, f32[16]{0:T(128)}, u32[]{:S(2)}) copy-start(f32[16]{0:T(128)} %copy-done.51) | copy-start | bytes 196
  214.7 99.1 %copy-start.47 = (f32[16]{0:T(128)S(1)}, f32[16]{0:T(128)}, u32[]{:S(2)}) copy-start(f32[16]{0:T(128)} %copy-done.46) | copy-start | bytes 196
  214.7 103.2 %copy-start.34 = (f32[768]{0:T(1024)S(1)}, f32[768]{0:T(1024)}, u32[]{:S(2)}) copy-start(f32[768]{0:T(1024)} %param.35) | copy-start | bytes 9220
  214.7 103.2 %copy-start.36 = (f32[1024]{0:T(1024)S(1)}, f32[1024]{0:T(1024)}, u32[]{:S(2)}) copy-start(f32[1024]{0:T(1024)} %copy-done.35) | copy-start | bytes 12292
  215.8 1280.4 %all-gather.3.cloned.1.call-start = ((), (), s32[]{:S(2)}) async-start(), calls=%async_computation.2 | async-start | bytes 14665728 | tf_op jit(solution)/shard_map/all_gather | solution.py:237
  317.9 4.5 copy-start.3
  323.4 14.4 slice-start.4
  327.5 10.3 slice-start.5
  327.5 10.3 copy-start.62
  327.5 22.8 %slice-start.8 = ((s8[4718592]{0:T(1024)(128)(4,1)}), s8[4194304]{0:T(1024)(128)(4,1)S(1)}, s32[]{:S(2)}) async-start(s8[4718592]{0:T(1024)(128)(4,1)} %bitcast.205), calls=%async_computation.11 | async-start | bytes 8388608
  337.9 12.5 copy-start.6
  337.9 12.5 slice-start.9
  350.4 6.5 copy-start.38
  366.9 3.1 copy-start.7
  374.6 6.9 slice-start
  375.0 6.5 slice-start.1
  375.1 6.5 copy-start.10
  386.1 4.9 copy-start.16
  416.2 3.9 copy-start.57
  429.2 3.9 copy-start.17
  429.2 6.3 copy-start.58
  502.7 22.9 %copy-start.50 = (f32[768]{0:T(1024)S(1)}, f32[768]{0:T(1024)}, u32[]{:S(2)}) copy-start(f32[768]{0:T(1024)} %get-tuple-element.32) | copy-start | bytes 9220
  502.7 24.2 %copy-start.49 = (f32[768]{0:T(1024)S(1)}, f32[768]{0:T(1024)}, u32[]{:S(2)}) copy-start(f32[768]{0:T(1024)} %get-tuple-element.37) | copy-start | bytes 9220
  528.2 80.3 %copy-start.43 = (f32[3072]{0:T(1024)S(1)}, f32[3072]{0:T(1024)}, u32[]{:S(2)}) copy-start(f32[3072]{0:T(1024)} %get-tuple-element.77) | copy-start | bytes 36868
  609.9 80.8 %copy-start.41 = (f32[768]{0:T(1024)S(1)}, f32[768]{0:T(1024)}, u32[]{:S(2)}) copy-start(f32[768]{0:T(1024)} %get-tuple-element.40) | copy-start | bytes 9220
  609.9 82.1 %copy-start.42 = (f32[768]{0:T(1024)S(1)}, f32[768]{0:T(1024)}, u32[]{:S(2)}) copy-start(f32[768]{0:T(1024)} %get-tuple-element.30) | copy-start | bytes 9220
  609.9 83.4 %copy-start.40 = (f32[768]{0:T(1024)S(1)}, f32[768]{0:T(1024)}, u32[]{:S(2)}) copy-start(f32[768]{0:T(1024)} %get-tuple-element.35) | copy-start | bytes 9220
  778.7 611.8 %copy-start.24 = (bf16[8,128,12,64]{1,0,3,2:T(8,128)(2,1)S(1)}, bf16[8,128,12,64]{1,0,3,2:T(8,128)(2,1)}, u32[]{:S(2)}) copy-start(bf16[8,128,12,64]{1,0,3,2:T(8,128)(2,1)} %copy-done.23) | copy-start | bytes 4718596
  1383.7 4.4 collective-permute-start
  1613.3 11.0 copy-start.1
  (32 other events, 63.4 us)
Sparse Core Ops, SparseCore 0:
  215.9 96.8 reduce-scatter.3
  1390.6 105.6 all-gather.2
where the time goes:
time: 1650 us; the launch traced here: 1630 us
  blocking collectives  727 us (44%)
  local copies, waits for them, and re-layouts  523 us (32%)
  waiting for transfers between devices  194 us (12%)
  matrix products  133 us (8%)
  other arithmetic  37.2 us (2%)
    unnamed x2, blocking collectives  614 us
    unnamed x181, local copies, waits for them, and re-layouts  317 us
    all_gather x1, waiting for transfers between devices, shards(): lax.all_gather(shares.astype(jnp.bfloat16), ('stream', 'dp'), axis=0, til...  96.9 us
    reduce_scatter x1, waiting for transfers between devices, shards(): lax.psum_scatter(grad_terms.reshape(2 * pairs_all, D), ('stream', 'dp'),...  93.5 us
    all_gather x1, blocking collectives, shards(): lax.all_gather(unit_rows, ('stream', 'dp'), axis=0, tiled=True)  69.7 us
    slice x6, local copies, waits for them, and re-layouts, shards(): summed.append(reduced[cursor:cursor + piece_len].reshape(piece.shape))  58 us
    psum x1, blocking collectives, shards(): counts = lax.psum(jnp.sum(own_hits, axis=0), 'dp')  43.5 us
    reshape x1, local copies, waits for them, and re-layouts, shards(): flat_grads = flat_grads.reshape(share_devices, share_count)  37.8 us
  transfers between devices with their start and end apart: 3, of which 3 were waited for; matrix products, arithmetic and copies ran while one was open for 1% of the time, Pallas kernels for 0%

commit v1 on v0

--- a/solution.py
+++ b/solution.py
@@ -124,7 +124,7 @@
     others = lax.dynamic_index_in_dim(everyone, 1 - half_index, 0, keepdims=False)
     group_range = jnp.arange(GROUPS, dtype=jnp.int32)
     own_hits = (pair_group[:, None] == group_range[None, :]).astype(jnp.float32)
-    counts = lax.psum(jnp.sum(own_hits, axis=0), "dp")
+    counts = jnp.sum(lax.all_gather(jnp.sum(own_hits, axis=0), "dp"), axis=0)
     row_weight = pairs_all / GROUPS / jnp.sum(own_hits * counts[None, :], axis=1)
     sim_scores = LOGIT_SCALE * jnp.einsum(
         "id,jd->ij", unit_rows, others, preferred_element_type=jnp.float32

time: 1650 us -> 1650 us (level)
    unnamed x2 -> x3, blocking collectives: 614 us -> 660 us
    psum x1 -> x0, blocking collectives: 43.5 us -> none  [shards(): counts = lax.psum(jnp.sum(own_hits, axis=0), 'dp')]
    unnamed x181 -> x183, local copies, waits for them, and re-layouts: 317 us -> 317 us
where the time goes in v1:
time: 1650 us; the launch traced here: 1630 us
  blocking collectives  728 us (44%)
  local copies, waits for them, and re-layouts  524 us (32%)
  waiting for transfers between devices  191 us (12%)
  matrix products  133 us (8%)
  other arithmetic  37.2 us (2%)
  between operations  16.7 us (1%)
    unnamed x3, blocking collectives  660 us
    unnamed x183, local copies, waits for them, and re-layouts  317 us
    all_gather x1, waiting for transfers between devices, shards(): lax.all_gather(shares.astype(jnp.bfloat16), ('stream', 'dp'), axis=0, til...  96.8 us
    reduce_scatter x1, waiting for transfers between devices, shards(): lax.psum_scatter(grad_terms.reshape(2 * pairs_all, D), ('stream', 'dp'),...  91.3 us
    all_gather x1, blocking collectives, shards(): lax.all_gather(unit_rows, ('stream', 'dp'), axis=0, tiled=True)  68 us
    slice x6, local copies, waits for them, and re-layouts, shards(): summed.append(reduced[cursor:cursor + piece_len].reshape(piece.shape))  58 us
    reshape x1, local copies, waits for them, and re-layouts, shards(): flat_grads = flat_grads.reshape(share_devices, share_count)  37.8 us
    dot_general x1, matrix products, shards(): jnp.dot(normed_low, up_weight, preferred_element_type=jnp.float32) + up_bias  34.5 us
  transfers between devices with their start and end apart: 3, of which 3 were waited for; matrix products, arithmetic and copies ran while one was open for 1% of the time, Pallas kernels for 0%

profile of v1, /device:TPU:0, one launch (start us, length us, event | category | flops | bytes accessed | tf_op | source)
XLA Modules:
  0.0 1631.4 jit_solution(14366901326113563180)
XLA Ops:
  11.9 16.7 %all-reduce.2 = s32[256]{0:T(256)} all-reduce(s32[256]{0:T(256)S(1)} %dynamic-update-slice.4), channel_id=1, replica_groups=mesh['stream'=2,'dp'=16] {'dp'}, use_global_device_ids=true, to_apply=%add.2 | all-reduce | flops 256 | bytes 2048
  28.8 38.6 %all-reduce.1 = f32[1744]{0:T(1024)S(1)} all-reduce(f32[1744]{0:T(1024)S(1)} %dynamic-update-slice.3), channel_id=2, replica_groups=mesh['stream'=2,'dp'=16] {'dp'}, use_global_device_ids=true, to_apply=%add.1 | all-reduce | flops 1744 | bytes 13952
  69.0 4.3 add_convert_fusion
  85.2 3.1 copy.99
  101.6 34.5 %fusion.3 = (bf16[1024,3072]{1,0:T(8,128)(2,1)S(1)}, f32[1024,3072]{1,0:T(8,128)}) fusion(f32[3072]{0:T(1024)S(1)} %copy-done.61, bf16[768,3072]{1,0:T(8,128)(2,1)S(1)} %bitcast.205, f32[1024,768]{1,0:T(8,128)S(1)} %get-tuple-element.63, f32[768]{0:T(1024)S(1)} %copy-done.37, f32[768]{0:T(1024)S(1)} %copy-done.32, f32[1024]{0:T(1024)S(1)} %add_rsqrt_fusion.1, ...), kind=kOutput, calls=%fused_computation.6 | convolution fusion | flops 5043388416 | bytes 26765312 | tf_op jit(solution)/shard_map/dot_general | solution.py:109
  136.2 5.5 fusion.100
  145.0 68.0 %all_gather.18 = bf16[512,768]{1,0:T(8,128)(2,1)S(1)} all-gather(bf16[16,768]{1,0:T(8,128)(2,1)S(1)} %fusion.71), channel_id=1, replica_groups=mesh['stream'=2,'dp'=16] {'stream','dp'}, dimensions={0}, use_global_device_ids=true | all-gather | bytes 811008 | tf_op jit(solution)/shard_map/all_gather | solution.py:119
  217.9 3.4 convert.3
  221.3 91.3 %reduce-scatter.4.cloned.1.call-done = f32[16,768]{1,0:T(8,128)} async-done(((f32[512,768]{1,0:T(8,128)}), f32[16,768]{1,0:T(8,128)}) %reduce-scatter.4.cloned.1.call-update) | async-done | bytes 49168 | tf_op jit(solution)/shard_map/reduce_scatter | solution.py:149
  317.7 4.5 fusion.19
  323.3 4.1 convert_reduce_fusion.1
  327.4 10.3 fusion.86
  337.7 12.5 convert_reduce_fusion
  350.2 6.5 multiply_reduce_fusion.1
  356.7 8.9 convolution_bitcast_fusion
  374.9 6.4 convert_reduce_fusion.3
  385.9 4.9 fusion.41
  393.0 10.8 reshape.345
  403.8 9.6 copy.134
  422.7 3.0 copy.120
  425.7 3.2 reshape.342
  429.0 3.9 copy.114
  438.2 3.0 copy.118
  441.2 3.2 reshape.340
  444.4 4.7 convolution_bitcast_fusion.2
  449.1 3.0 copy.119
  452.1 3.2 reshape.341
  455.4 3.3 constant_dynamic-update-slice_fusion.9
  460.0 21.2 %dynamic-update-slice.7 = f32[7087104]{0:T(1024)} dynamic-update-slice(f32[7087104]{0:T(1024)} %constant_dynamic-update-slice_fusion.8, f32[589824]{0:T(1024)} %reshape.341, s32[]{} %constant.186) | dynamic-update-slice | bytes 4718596
  481.2 21.2 %dynamic-update-slice.8 = f32[7087104]{0:T(1024)} dynamic-update-slice(f32[7087104]{0:T(1024)} %dynamic-update-slice.7, f32[589824]{0:T(1024)} %reshape.342, s32[]{} %constant.187) | dynamic-update-slice | bytes 4718596
  503.7 20.2 %dynamic-update-slice.10 = f32[7087104]{0:T(1024)} dynamic-update-slice(f32[7087104]{0:T(1024)} %constant_dynamic-update-slice_fusion.7, f32[589824]{0:T(1024)S(1)} %reshape.343, s32[]{} %constant.189) | dynamic-update-slice | bytes 4718596
  527.8 80.6 %dynamic-update-slice.14 = f32[7087104]{0:T(1024)} dynamic-update-slice(f32[7087104]{0:T(1024)} %constant_dynamic-update-slice_fusion.4, f32[2359296]{0:T(1024)} %bitcast.173, s32[]{} %constant.193) | dynamic-update-slice | bytes 18874372
  609.7 80.7 %dynamic-update-slice.16 = f32[7087104]{0:T(1024)} dynamic-update-slice(f32[7087104]{0:T(1024)} %constant_dynamic-update-slice_fusion.3, f32[2359296]{0:T(1024)} %reshape.345, s32[]{} %constant.195) | dynamic-update-slice | bytes 18874372
  694.4 37.8 %reshape.346 = f32[32,221472]{1,0:T(8,128)} reshape(f32[7087104]{0:T(1024)} %constant_dynamic-update-slice_fusion) | data formatting | bytes 56696832 | tf_op jit(solution)/shard_map/reshape | solution.py:234
  732.2 20.9 %pad.6 = f32[32,221568]{1,0:T(8,128)} pad(f32[32,221472]{1,0:T(8,128)} %reshape.346, f32[]{:T(128)} %constant.120.clone.1), padding=0_0x0_96 | pad | bytes 56709124 | tf_op jit(solution)/shard_map/jit(_pad)/pad | solution.py:235
  753.1 25.4 %reshape.347 = f32[55392,128]{1,0:T(8,128)} reshape(f32[32,221568]{1,0:T(8,128)} %pad.6) | data formatting | bytes 56721408 | tf_op jit(solution)/shard_map/reshape | solution.py:235
  778.5 605.0 %fusion = f32[1744,128]{1,0:T(8,128)S(1)} fusion(f32[55392,128]{1,0:T(8,128)} %reshape.347), kind=kCustom, calls=%all-reduce-scatter | all-reduce-scatter fusion | flops 7143425 | bytes 29253632
  1384.9 3.1 collective-permute-done
  1395.9 3.3 add_bitcast_fusion
  1399.2 96.8 %all-gather.4.cloned.1.call-done = bf16[32,1731,128]{2,1,0:T(8,128)(2,1)} async-done(((bf16[1,1731,128]{2,1,0:T(8,128)(2,1)}), bf16[32,1731,128]{2,1,0:T(8,128)(2,1)}) %all-gather.4.cloned.1.call-update) | async-done | bytes 14180368 | tf_op jit(solution)/shard_map/all_gather | solution.py:237
  1496.0 12.8 copy.209
  1508.8 9.7 slice_convert_fusion
  1518.6 36.5 %reshape.367 = f32[7087104]{0:T(1024)} reshape(f32[32,221472]{1,0:T(8,128)} %slice_convert_fusion) | data formatting | bytes 56696832
  1557.8 8.3 slice.115
  1566.1 31.3 %slice.87 = f32[9228,768]{1,0:T(8,128)} reshape(f32[7087104]{0:T(1024)} %reshape.367) | data formatting | bytes 56696832 | tf_op jit(solution)/shard_map/slice | solution.py:245
  1597.4 8.1 slice.117
  1605.5 7.7 fusion.97
  1613.1 11.0 reshape.350
  (247 shorter events, 98.3 us)
Async XLA Ops:
  7.2 89.9 %copy-start = (bf16[768,768]{1,0:T(8,128)(2,1)S(1)}, bf16[768,768]{1,0:T(8,128)(2,1)}, u32[]{:S(2)}) copy-start(bf16[768,768]{1,0:T(8,128)(2,1)} %param.27) | copy-start | bytes 3538948
  7.2 305.4 %reduce-scatter.4.cloned.1.call-start = ((), (), s32[]{:S(2)}) async-start(), calls=%async_computation.1 | async-start | bytes 1622016 | tf_op jit(solution)/shard_map/reduce_scatter | solution.py:149
  69.0 24.6 %copy-start.29 = (pred[128,128]{0,1:T(8,128)(4,1)}, pred[128,128]{0,1:T(8,128)(4,1)S(1)}, u32[]{:S(2)}) copy-start(pred[128,128]{0,1:T(8,128)(4,1)S(1)} %broadcast_compare_fusion) | copy-start | bytes 49156
  73.3 3.4 copy-start.63
  82.7 11.0 copy-start.9
  97.2 38.9 %slice-start.2 = ((s8[4718592]{0:T(1024)(128)(4,1)}), s8[4194304]{0:T(1024)(128)(4,1)S(1)}, s32[]{:S(2)}) async-start(s8[4718592]{0:T(1024)(128)(4,1)} %bitcast.200), calls=%async_computation.5 | async-start | bytes 8388608
  99.0 37.2 %copy-start.5 = (f32[1024,768]{1,0:T(8,128)}, f32[1024,768]{1,0:T(8,128)S(1)}, u32[]{:S(2)}) copy-start(f32[1024,768]{1,0:T(8,128)S(1)} %get-tuple-element.63) | copy-start | bytes 9437188
  101.6 34.6 %slice-start.3 = ((s8[4718592]{0:T(1024)(128)(4,1)}), s8[524288]{0:T(1024)(128)(4,1)S(1)}, s32[]{:S(2)}) async-start(s8[4718592]{0:T(1024)(128)(4,1)} %bitcast.200), calls=%async_computation.6 | async-start | bytes 1048576
  101.6 34.6 %copy-start.65 = (f32[768]{0:T(1024)S(1)}, f32[768]{0:T(1024)}, u32[]{:S(2)}) copy-start(f32[768]{0:T(1024)} %param.34) | copy-start | bytes 9220
  136.2 5.5 copy-start.66
  142.5 70.5 %copy-start.39 = (s32[256]{0:T(256)S(1)}, s32[256]{0:T(256)}, u32[]{:S(2)}) copy-start(s32[256]{0:T(256)} %all-reduce.2) | copy-start | bytes 3076
  142.5 70.5 %copy-start.44 = (s32[16]{0:T(128)S(1)}, s32[16]{0:T(128)}, u32[]{:S(2)}) copy-start(s32[16]{0:T(128)} %param.21) | copy-start | bytes 196
  142.5 70.5 %copy-start.45 = (s32[16]{0:T(128)S(1)}, s32[16]{0:T(128)}, u32[]{:S(2)}) copy-start(s32[16]{0:T(128)} %iota_add_fusion) | copy-start | bytes 196
  142.5 71.1 %copy-start.53 = (f32[16]{0:T(128)S(1)}, f32[16]{0:T(128)}, u32[]{:S(2)}) copy-start(f32[16]{0:T(128)} %select_reduce_fusion.1) | copy-start | bytes 196
  144.3 69.8 %copy-start.18 = (f32[16,1,768]{2,1,0:T(1,128)}, f32[16,1,768]{2,1,0:T(1,128)S(1)}, u32[]{:S(2)}) copy-start(f32[16,1,768]{2,1,0:T(1,128)S(1)} %slice.104) | copy-start | bytes 147460
  145.0 69.2 %copy-start.46 = (f32[16]{0:T(128)}, f32[16]{0:T(128)S(1)}, u32[]{:S(2)}) copy-start(f32[16]{0:T(128)S(1)} %add_rsqrt_fusion.2) | copy-start | bytes 196
  145.0 69.1 %copy-start.31 = (bf16[16,768]{1,0:T(8,128)(2,1)}, bf16[16,768]{1,0:T(8,128)(2,1)S(1)}, u32[]{:S(2)}) copy-start(bf16[16,768]{1,0:T(8,128)(2,1)S(1)} %fusion.71) | copy-start | bytes 73732
  216.7 95.9 %copy-start.19 = (f32[16,1,768]{2,1,0:T(1,128)S(1)}, f32[16,1,768]{2,1,0:T(1,128)}, u32[]{:S(2)}) copy-start(f32[16,1,768]{2,1,0:T(1,128)} %copy-done.18) | copy-start | bytes 147460
  216.7 96.8 %copy-start.52 = (f32[16]{0:T(128)S(1)}, f32[16]{0:T(128)}, u32[]{:S(2)}) copy-start(f32[16]{0:T(128)} %copy-done.51) | copy-start | bytes 196
  216.7 96.8 %copy-start.47 = (f32[16]{0:T(128)S(1)}, f32[16]{0:T(128)}, u32[]{:S(2)}) copy-start(f32[16]{0:T(128)} %copy-done.46) | copy-start | bytes 196
  216.7 101.0 %copy-start.34 = (f32[768]{0:T(1024)S(1)}, f32[768]{0:T(1024)}, u32[]{:S(2)}) copy-start(f32[768]{0:T(1024)} %param.35) | copy-start | bytes 9220
  216.7 101.0 %copy-start.36 = (f32[1024]{0:T(1024)S(1)}, f32[1024]{0:T(1024)}, u32[]{:S(2)}) copy-start(f32[1024]{0:T(1024)} %copy-done.35) | copy-start | bytes 12292
  217.9 1278.2 %all-gather.4.cloned.1.call-start = ((), (), s32[]{:S(2)}) async-start(), calls=%async_computation.2 | async-start | bytes 14665728 | tf_op jit(solution)/shard_map/all_gather | solution.py:237
  317.7 4.5 copy-start.3
  323.3 14.4 slice-start.4
  327.4 10.3 slice-start.5
  327.4 10.3 copy-start.62
  327.4 22.8 %slice-start.8 = ((s8[4718592]{0:T(1024)(128)(4,1)}), s8[4194304]{0:T(1024)(128)(4,1)S(1)}, s32[]{:S(2)}) async-start(s8[4718592]{0:T(1024)(128)(4,1)} %bitcast.206), calls=%async_computation.11 | async-start | bytes 8388608
  337.7 12.5 copy-start.6
  337.7 12.5 slice-start.9
  350.2 6.5 copy-start.38
  366.8 3.1 copy-start.7
  374.4 6.9 slice-start
  374.9 6.5 slice-start.1
  374.9 6.5 copy-start.10
  385.9 4.9 copy-start.16
  416.0 3.9 copy-start.57
  429.0 3.9 copy-start.17
  429.0 6.3 copy-start.58
  502.4 22.8 %copy-start.50 = (f32[768]{0:T(1024)S(1)}, f32[768]{0:T(1024)}, u32[]{:S(2)}) copy-start(f32[768]{0:T(1024)} %get-tuple-element.32) | copy-start | bytes 9220
  502.4 24.1 %copy-start.49 = (f32[768]{0:T(1024)S(1)}, f32[768]{0:T(1024)}, u32[]{:S(2)}) copy-start(f32[768]{0:T(1024)} %get-tuple-element.37) | copy-start | bytes 9220
  527.8 80.6 %copy-start.43 = (f32[3072]{0:T(1024)S(1)}, f32[3072]{0:T(1024)}, u32[]{:S(2)}) copy-start(f32[3072]{0:T(1024)} %get-tuple-element.77) | copy-start | bytes 36868
  609.7 80.8 %copy-start.41 = (f32[768]{0:T(1024)S(1)}, f32[768]{0:T(1024)}, u32[]{:S(2)}) copy-start(f32[768]{0:T(1024)} %get-tuple-element.40) | copy-start | bytes 9220
  609.7 82.1 %copy-start.42 = (f32[768]{0:T(1024)S(1)}, f32[768]{0:T(1024)}, u32[]{:S(2)}) copy-start(f32[768]{0:T(1024)} %get-tuple-element.30) | copy-start | bytes 9220
  609.7 83.4 %copy-start.40 = (f32[768]{0:T(1024)S(1)}, f32[768]{0:T(1024)}, u32[]{:S(2)}) copy-start(f32[768]{0:T(1024)} %get-tuple-element.35) | copy-start | bytes 9220
  778.5 611.8 %copy-start.24 = (bf16[8,128,12,64]{1,0,3,2:T(8,128)(2,1)S(1)}, bf16[8,128,12,64]{1,0,3,2:T(8,128)(2,1)}, u32[]{:S(2)}) copy-start(bf16[8,128,12,64]{1,0,3,2:T(8,128)(2,1)} %copy-done.23) | copy-start | bytes 4718596
  1383.6 4.4 collective-permute-start
  1613.1 11.0 copy-start.1
  (32 other events, 63.3 us)
Sparse Core Ops, SparseCore 0:
  218.0 94.5 reduce-scatter.3
  1390.4 105.5 all-gather.3
